TPU v7x, 256 devices: a whole 4x4x8 slice. The times are simulated.
256 devices in a mesh: dp: 16 (over x, z_hi), mp: 16 (over z_lo, y, core).
Axes of the slice: x: 4, y: 4, z: 8 (z_hi: 4, z_lo: 2; z = z_hi * 2 + z_lo), core: 2. Of those that a mesh axis runs over, the one named last changes fastest.
Arguments:
- features: bfloat16 [16, 320, 128, 128], P('dp', 'mp'), may hold values from -6 to 6
- w_out: bfloat16 [320, 36], P('mp'), may hold values from -0.109375 to 0.109375
- noisy_latent: float32 [16, 4, 128, 128], P('dp', None, 'mp'), may hold values from -6 to 6
- timestep: int32 [16], P('dp'), may hold values from 100 to 699
- w_in: bfloat16 [9, 512, 4], replicated, may hold values from -1 to 1
- b_in: float32 [512], replicated, may hold values from -3 to 3
- w_mid: bfloat16 [9, 512, 512], replicated, may hold values from -0.09375 to 0.09375
- b_mid: float32 [512], replicated, may hold values from -3 to 3
- reward_head: float32 [512], replicated, may hold values from -6 to 6
Outputs:
- feature_grads: bfloat16 [16, 320, 128, 128], P('dp', 'mp')
- weight_grad: float32 [320, 36], P('mp')
All inputs are finite; a program needn't handle non-finite values.
Results may differ from a plain program's by a relative error of at most 0.012.
Values may be sent and summed in bfloat16 or wider, within the bound.
A program may use at most 128 MiB of HBM per device.

v0:
```python
import jax
import jax.numpy as jnp
import numpy as np
from jax import lax
from jax.experimental import pallas as pl
from jax.experimental.pallas import tpu as pltpu
from jax.sharding import PartitionSpec as P

F32 = jnp.float32
BF16 = jnp.bfloat16
MESH = pl.DeviceIdType.MESH
N = 16
STRIDE = 136
CHUNK = 1024
NT = (((1,), (1,)), ((), ()))


def noise_table():
    betas = np.linspace(0.00085**0.5, 0.012**0.5, 1000, dtype=np.float32) ** 2
    table = np.cumprod((1.0 - betas).astype(np.float32), dtype=np.float32)
    return np.pad(table, (0, 24)).reshape(8, 128)


def iota(shape, dim):
    return lax.broadcasted_iota(jnp.int32, shape, dim)


def dot(a, b):
    return jnp.dot(a, b, preferred_element_type=F32)


def dot_nt(a, b):
    return lax.dot_general(a, b, NT, preferred_element_type=F32)


def right(v):
    return jnp.where(iota(v.shape, 1) == 0, 0.0, pltpu.roll(v, 1, 1))


def left(v):
    return jnp.where(iota(v.shape, 1) == 127, 0.0, pltpu.roll(v, 127, 1))


def rows(start, size):
    return pl.ds(pl.multiple_of(start, size), size)


def each(lo, hi, step):
    def run(j, c):
        step(j)
        return c

    lax.fori_loop(lo, hi, run, 0)


def kernel(
    feat, w_out, noisy, tstep, table, w_in, b_in, w_mid, b_mid, head,
    fg_out, wg_out,
    fbuf, wobuf, nbuf, tbuf, tabbuf, wibuf, bibuf, wmbuf, bmbuf, hbuf,
    stage, f2, rs, eacc, nz, eloc, recv, e48, e48t, w48, ls,
    h3, s1, m3, gacc, lacc, ngblk, grecv, ns, im, fgb, wgb, wrecv,
    in_sem, out_sem, send_sem, recv_sem, gsend_sem, grecv_sem, wsend_sem, wrecv_sem,
):
    me = lax.axis_index("mp")
    my_dp = lax.axis_index("dp")
    pairs = ((feat, fbuf), (w_out, wobuf), (noisy, nbuf), (tstep, tbuf), (table, tabbuf),
             (w_in, wibuf), (b_in, bibuf), (b_mid, bmbuf), (head, hbuf), (w_mid, wmbuf))
    loads = [pltpu.make_async_copy(src, dst, in_sem.at[i]) for i, (src, dst) in enumerate(pairs)]
    for copy in loads:
        copy.start()
    barrier = pltpu.get_barrier_semaphore()

    def greet(j):
        pl.semaphore_signal(barrier, inc=1, device_id={"mp": lax.rem(me + j, N)}, device_id_type=MESH)
        pl.semaphore_signal(barrier, inc=1, device_id={"dp": lax.rem(my_dp + j, N)}, device_id_type=MESH)

    each(1, N, greet)

    for copy in loads[1:5]:
        copy.wait()
    level = jnp.sum(
        jnp.where(iota((8, 128), 0) * 128 + iota((8, 128), 1) == tbuf[0], tabbuf[...], 0.0), keepdims=True
    )
    root_a = jnp.sqrt(level)
    root_b = jnp.sqrt(1.0 - level)
    ratio = root_b / root_a

    def tap_column(b):
        j = lax.shift_right_logical(b, 2) & 3
        k = 3 * (2 - j) + lax.shift_right_logical(b, 4)
        return jnp.where(j < 3, 4 * k + (b & 3), -1)

    pick = jnp.where(iota((36, 48), 0) == tap_column(iota((36, 48), 1)), 1.0, 0.0).astype(BF16)
    pick_t = jnp.where(iota((48, 36), 1) == tap_column(iota((48, 36), 0)), 1.0, 0.0).astype(BF16)
    e48t[...] = jnp.zeros((32, 48), F32)
    e48t[0:20, :] = dot(wobuf[...], pick)
    e48[...] = jnp.zeros((48, 32), F32)
    e48[:, 0:20] = dot_nt(pick_t, wobuf[...])

    loads[0].wait()
    for c in range(20):
        stage[c * STRIDE : c * STRIDE + 128, :] = fbuf[0, c].astype(F32)
    for c in range(20, 24):
        stage[c * STRIDE : c * STRIDE + 128, :] = jnp.zeros((128, 128), F32)
    rs[0:16, :] = jnp.zeros((16, 128), F32)
    rs[129 * 16 : 130 * 16, :] = jnp.zeros((16, 128), F32)
    e_rows = e48[...].astype(BF16)

    def unet_rows(b):
        parts = []
        for i in range(CHUNK // 128):
            v = stage[pl.ds(b * (CHUNK // 128) + i, 24, stride=STRIDE), :]
            parts.append(jnp.concatenate([v, jnp.zeros((8, 128), F32)], axis=0).astype(BF16))
        block = jnp.concatenate(parts, axis=1)
        f2[:, rows(b * CHUNK, CHUNK)] = block
        p = dot(e_rows, block)
        for i in range(CHUNK // 128):
            q = p[:, i * 128 : (i + 1) * 128]
            y = b * (CHUNK // 128) + i
            rs[rows((y + 1) * 16, 16), :] = q[16:32] + right(q[0:16]) + left(q[32:48])

    each(0, 16384 // CHUNK, unet_rows)

    for o in range(4):
        nz[pl.ds(o, 8, stride=4), :] = nbuf[0, o]
    eacc[0:8, :] = jnp.zeros((8, 128), F32)
    eacc[520:528, :] = jnp.zeros((8, 128), F32)
    low = iota((8, 128), 0) < 4

    def unet_pairs(b):
        def at(y, half):
            return rs[rows((y + 1) * 16 + 8 * half, 8), :]

        for i in range(4):
            y = 8 * b + 2 * i
            e = at(y + 1, 0)
            e += jnp.where(low, pltpu.roll(at(y, 0), 4, 0), pltpu.roll(at(y, 1), 4, 0))
            e += jnp.where(low, at(y - 1, 1), pltpu.roll(at(y + 2, 0), 4, 0))
            eacc[rows(8 + 4 * y, 8), :] = -ratio * e

    each(0, 16, unet_pairs)
    mine = pl.ds(pl.multiple_of(8 + 32 * me, 8), 32)
    eacc[mine, :] = eacc[mine, :] + nz[...] / root_a
    eloc[...] = eacc[...].astype(BF16)

    def lat_copy(dest, slot):
        return pltpu.make_async_remote_copy(
            src_ref=eloc.at[pl.ds(pl.multiple_of(32 * dest, 32), 48), :],
            dst_ref=recv.at[slot],
            send_sem=send_sem.at[slot],
            recv_sem=recv_sem.at[slot],
            device_id={"mp": dest},
            device_id_type=MESH,
        )

    pl.semaphore_wait(barrier, 2 * (N - 1))
    each(1, N, lambda j: lat_copy(lax.rem(me + j, N), j).start())

    loads[5].wait()
    loads[6].wait()
    w_rows = jnp.zeros((48, 512), F32)
    for k in range(9):
        ky, kx = divmod(k, 3)
        put = jnp.where(iota((48, 4), 0) == kx * 16 + ky * 4 + iota((48, 4), 1), 1.0, 0.0).astype(BF16)
        w_rows = w_rows + dot_nt(put, wibuf[k])
    w48[...] = w_rows.astype(BF16)
    for copy in loads[7:]:
        copy.wait()

    total = eacc[pl.ds(pl.multiple_of(32 * me, 32), 48), :]

    def lat_take(j, acc):
        lat_copy(lax.rem(me + j, N), j).wait_recv()
        return acc + recv[j].astype(F32)

    total = lax.fori_loop(1, N, lat_take, total)

    lat = total.astype(BF16).astype(F32)
    for i, t in enumerate((right(lat), lat, left(lat))):
        ls[i, 0:48, :] = t
        ls[i, 48:56, :] = jnp.zeros((8, 128), F32)
    edge = iota((128, 512), 0)
    first, last = edge == 0, edge == 127

    def spread(dst, r, val, down, up):
        at = rows(r * 128, 128)
        dst[at, down * 512 : down * 512 + 512] = jnp.where(first, 0.0, pltpu.roll(val, 1, 0)).astype(BF16)
        dst[at, 512:1024] = val.astype(BF16)
        dst[at, up * 512 : up * 512 + 512] = jnp.where(last, 0.0, pltpu.roll(val, 127, 0)).astype(BF16)

    def hidden(r):
        at = pl.ds(4 * r, 16)
        x48 = jnp.concatenate([ls[0, at, :], ls[1, at, :], ls[2, at, :]], axis=0)
        pre = dot(x48.T.astype(BF16), w48[...]) + bibuf[...]
        row = 8 * me - 1 + r
        half = jnp.where(jnp.logical_and(row >= 0, row < 128), 0.5, 0.0)
        sig = half * jnp.tanh(0.5 * pre) + half
        act = pre * sig
        s1[rows(r * 128, 128), :] = sig + act * (1.0 - sig)
        spread(h3, r, act, 0, 2)

    each(0, 10, hidden)

    def mixed(b):
        acc = jnp.broadcast_to(bmbuf[...], (4 * 128, 512))
        for ky in range(3):
            for kx in range(3):
                a = h3[pl.ds(pl.multiple_of((b * 4 + ky) * 128, 128), 4 * 128), kx * 512 : kx * 512 + 512]
                acc = acc + dot_nt(a, wmbuf[3 * ky + kx])
        for i in range(4):
            pre = acc[i * 128 : (i + 1) * 128]
            sig = 0.5 * jnp.tanh(0.5 * pre) + 0.5
            spread(m3, b * 4 + i, hbuf[...] * (sig + (pre * sig) * (1.0 - sig)), 2, 0)

    each(0, 8 // 4, mixed)

    gacc[1024:1280, :] = jnp.zeros((256, 512), F32)
    for ky in range(3):
        g = dot(m3[...], wmbuf[3 * ky : 3 * ky + 3].reshape(1536, 512))
        at = pl.ds(ky * 128, 1024)
        gacc[at, :] = g if ky == 0 else gacc[at, :] + g
    lacc[...] = jnp.zeros((56, 128), F32)

    def latent_rows(r):
        at = rows(r * 128, 128)
        g = (gacc[at, :] * s1[at, :]).astype(BF16)
        q = dot_nt(w48[...], g)
        at = pl.ds(4 * r, 16)
        lacc[at, :] = lacc[at, :] + (q[16:32] + left(q[0:16]) + right(q[32:48]))

    each(0, 10, latent_rows)
    ngblk[...] = (-ratio * lacc[0:48, :]).astype(BF16)

    def ng_copy(peer, slot):
        return pltpu.make_async_remote_copy(
            src_ref=ngblk,
            dst_ref=grecv.at[slot],
            send_sem=gsend_sem.at[peer],
            recv_sem=grecv_sem.at[slot],
            device_id={"mp": peer},
            device_id_type=MESH,
        )

    def ng_take(j):
        peer = lax.rem(me + j, N)
        ng_copy(peer, peer).wait_recv()

    each(1, N, lambda j: ng_copy(lax.rem(me + j, N), me).start())
    grecv[me] = ngblk[...]
    ns[:, 0:8, :] = jnp.zeros((3, 8, 128), F32)
    ns[:, 512:528, :] = jnp.zeros((3, 16, 128), F32)
    each(1, N, ng_take)

    def shift(s, c):
        at = pl.ds(4 + 32 * s, 32)
        v = grecv[s].astype(F32)
        above = jnp.where(s > 0, grecv[jnp.maximum(s - 1, 0), 40 - 8 : 48].astype(F32)[8:16], 0.0)
        below = jnp.where(s < N - 1, grecv[jnp.minimum(s + 1, N - 1), 0:16].astype(F32)[0:8], 0.0)
        v = jnp.concatenate([v[8:16] + above, v[16:32], v[32:40] + below], axis=0)
        ns[0, at, :] = left(v)
        ns[1, at, :] = v
        ns[2, at, :] = right(v)
        return c

    lax.fori_loop(0, N, shift, 0)

    def columns(b, acc):
        parts = []
        for i in range(CHUNK // 128):
            at = pl.ds(4 * (b * (CHUNK // 128) + i), 16)
            parts.append(jnp.concatenate([ns[k, at, :].astype(BF16) for k in range(3)], axis=0))
        block = jnp.concatenate(parts, axis=1)
        at = rows(b * CHUNK, CHUNK)
        im[:, at] = block
        return acc + dot_nt(f2[:, at], block)

    wg = lax.fori_loop(0, 16384 // CHUNK, columns, jnp.zeros((32, 48), F32))
    wg = jnp.concatenate([wg[0:24], jnp.zeros((24, 80), F32)], axis=1)
    lane = iota((24, 128), 1)
    ordered = jnp.zeros((24, 128), F32)
    for k in range(9):
        ky, kx = divmod(k, 3)
        moved = pltpu.roll(wg, (4 * k - kx * 16 - (2 - ky) * 4) % 128, 1)
        ordered = jnp.where(jnp.logical_and(lane >= 4 * k, lane < 4 * k + 4), moved, ordered)
    wrecv[my_dp] = ordered[0:8] + pltpu.roll(ordered[8:16], 40, 1) + pltpu.roll(ordered[16:24], 80, 1)

    def wg_copy(peer, slot):
        return pltpu.make_async_remote_copy(
            src_ref=wrecv.at[my_dp],
            dst_ref=wrecv.at[slot],
            send_sem=wsend_sem.at[peer],
            recv_sem=wrecv_sem.at[slot],
            device_id={"dp": peer},
            device_id_type=MESH,
        )

    def wg_take(j):
        peer = lax.rem(my_dp + j, N)
        wg_copy(peer, peer).wait_recv()

    each(1, N, lambda j: wg_copy(lax.rem(my_dp + j, N), my_dp).start())

    e_cols = e48t[...].astype(BF16)

    def feature(b):
        p = dot(e_cols, im[:, rows(b * CHUNK, CHUNK)])
        for i in range(CHUNK // 128):
            stage[pl.ds(b * (CHUNK // 128) + i, 24, stride=STRIDE), :] = p[0:24, i * 128 : (i + 1) * 128]

    each(0, 16384 // CHUNK, feature)
    for c in range(20):
        fgb[0, c] = stage[c * STRIDE : c * STRIDE + 128, :].astype(BF16)
    fg_store = pltpu.make_async_copy(fgb, fg_out, out_sem.at[0])
    fg_store.start()
    each(1, N, wg_take)
    acc = wrecv[0]
    for s in range(1, N):
        acc = acc + wrecv[s]
    acc = acc * (1.0 / 16384.0)
    wgb[0:8, :] = acc[:, 0:36]
    wgb[8:16, :] = pltpu.roll(acc, 88, 1)[:, 0:36]
    wgb[16:20, :] = pltpu.roll(acc, 48, 1)[0:4, 0:36]
    wg_store = pltpu.make_async_copy(wgb, wg_out, out_sem.at[1])
    wg_store.start()

    def sent(j):
        lat_copy(lax.rem(me + j, N), j).wait_send()
        ng_copy(lax.rem(me + j, N), me).wait_send()
        wg_copy(lax.rem(my_dp + j, N), my_dp).wait_send()

    each(1, N, sent)
    fg_store.wait()
    wg_store.wait()


def body(features, w_out, noisy_latent, timestep, w_in, b_in, w_mid, b_mid, reward_head):
    hbm = pl.BlockSpec(memory_space=pltpu.HBM)
    dma = pltpu.SemaphoreType.DMA
    return pl.pallas_call(
        kernel,
        out_shape=(
            jax.ShapeDtypeStruct((1, 20, 128, 128), BF16),
            jax.ShapeDtypeStruct((20, 36), F32),
        ),
        in_specs=[hbm] * 10,
        out_specs=(hbm, hbm),
        scratch_shapes=[
            pltpu.VMEM((1, 20, 128, 128), BF16),
            pltpu.VMEM((20, 36), BF16),
            pltpu.VMEM((1, 4, 8, 128), F32),
            pltpu.SMEM((1,), jnp.int32),
            pltpu.VMEM((8, 128), F32),
            pltpu.VMEM((9, 512, 4), BF16),
            pltpu.VMEM((1, 512), F32),
            pltpu.VMEM((9, 512, 512), BF16),
            pltpu.VMEM((1, 512), F32),
            pltpu.VMEM((1, 512), F32),
            pltpu.VMEM((24 * STRIDE, 128), F32),
            pltpu.VMEM((32, 16384), BF16),
            pltpu.VMEM((130 * 16, 128), F32),
            pltpu.VMEM((528, 128), F32),
            pltpu.VMEM((32, 128), F32),
            pltpu.VMEM((528, 128), BF16),
            pltpu.VMEM((N, 48, 128), BF16),
            pltpu.VMEM((48, 32), F32),
            pltpu.VMEM((32, 48), F32),
            pltpu.VMEM((48, 512), BF16),
            pltpu.VMEM((3, 56, 128), F32),
            pltpu.VMEM((10 * 128, 1536), BF16),
            pltpu.VMEM((10 * 128, 512), F32),
            pltpu.VMEM((8 * 128, 1536), BF16),
            pltpu.VMEM((10 * 128, 512), F32),
            pltpu.VMEM((56, 128), F32),
            pltpu.VMEM((48, 128), BF16),
            pltpu.VMEM((N, 48, 128), BF16),
            pltpu.VMEM((3, 528, 128), F32),
            pltpu.VMEM((48, 16384), BF16),
            pltpu.VMEM((1, 20, 128, 128), BF16),
            pltpu.VMEM((20, 36), F32),
            pltpu.VMEM((N, 8, 128), F32),
            dma((10,)), dma((2,)), dma((N,)), dma((N,)), dma((N,)), dma((N,)), dma((N,)), dma((N,)),
        ],
        compiler_params=pltpu.CompilerParams(collective_id=0, has_side_effects=True, vmem_limit_bytes=56 << 20),
        name="step",
    )(
        features, w_out, noisy_latent, timestep, jnp.asarray(noise_table()), w_in,
        b_in.reshape(1, 512), w_mid, b_mid.reshape(1, 512), reward_head.reshape(1, 512),
    )


def solution(mesh):
    in_specs = (
        P("dp", "mp", None, None), P("mp", None), P("dp", None, "mp", None), P("dp"), P(), P(), P(), P(), P(),
    )
    out_specs = (P("dp", "mp", None, None), P("mp", None))
    return jax.shard_map(body, mesh=mesh, in_specs=in_specs, out_specs=out_specs, check_vma=False)
```

profile of v0, /device:TPU:1, one launch (start us, length us, event | category | flops | bytes accessed | tf_op | source)
XLA Modules:
  0.0 57.0 jit_solution(7304018097136920924)
XLA Ops:
  1.3 2.2 %copy.12.w_in = bf16[9,512,4]{2,1,0:T(8,128)(2,1)} copy(bf16[9,512,4]{1,2,0:T(4,128)(2,1)} %param.14) | data formatting | bytes 73728 | tf_op args[4]
  3.5 50.2 %step.1 = (bf16[1,20,128,128]{3,2,1,0:T(8,128)(2,1)}, f32[20,36]{1,0:T(8,128)}) custom-call(bf16[1,20,128,128]{3,2,1,0:T(8,128)(2,1)} %feat.1, bf16[20,36]{1,0:T(8,128)(2,1)} %w_out.1, f32[1,4,8,128]{3,2,1,0:T(8,128)} %noisy.1, s32[1]{0:T(128)S(6)} %copy.15.tstep, f32[8,128]{1,0:T(8,128)} %constant.2.clone.table, bf16[9,512,4]{2,1,0:T(8,128)(2,1)} %copy.12.w_in, ...), custom_call_target="tpu_custom_call" | custom-call | tf_op jit(solution)/shard_map/step/pallas_call | solution.py:339
  53.7 2.0 %copy.16 = bf16[1,20,128,128]{3,2,1,0:T(8,128)(2,1)} copy(bf16[1,20,128,128]{3,2,1,0:T(8,128)(2,1)} %get-tuple-element.4) | data formatting | bytes 1310720
  55.7 1.3 %copy.17 = f32[20,36]{1,0:T(8,128)} copy(f32[20,36]{1,0:T(8,128)} %get-tuple-element.5) | data formatting | bytes 5760
where the time goes:
time: 57.2 us; the launch traced here: 57 us
  Pallas kernels  50.2 us (88%)
  local copies, waits for them, and re-layouts  5.53 us (10%)
  between operations  1.29 us (2%)
    pallas_call x1, Pallas kernels, body(): pl.pallas_call(kernel, out_shape=(jax.ShapeDtypeStruct((1, 20, 128, 128),...  50.2 us
    unnamed x3, local copies, waits for them, and re-layouts  5.53 us

commit v1 on v0

--- a/solution.py
+++ b/solution.py
@@ -45,12 +45,12 @@
     return pl.ds(pl.multiple_of(start, size), size)
 
 
-def each(lo, hi, step):
+def each(lo, hi, step, unroll=1):
     def run(j, c):
         step(j)
         return c
 
-    lax.fori_loop(lo, hi, run, 0)
+    lax.fori_loop(lo, hi, run, 0, unroll=unroll)
 
 
 def kernel(
@@ -58,8 +58,8 @@
     fg_out, wg_out,
     fbuf, wobuf, nbuf, tbuf, tabbuf, wibuf, bibuf, wmbuf, bmbuf, hbuf,
     stage, f2, rs, eacc, nz, eloc, recv, e48, e48t, w48, ls,
-    h3, s1, m3, gacc, lacc, ngblk, grecv, ns, im, fgb, wgb, wrecv,
-    in_sem, out_sem, send_sem, recv_sem, gsend_sem, grecv_sem, wsend_sem, wrecv_sem,
+    h3, s1, m3, gacc, lacc, ngblk, grecv, ns, im, wrecv,
+    in_sem, send_sem, recv_sem, gsend_sem, grecv_sem, wsend_sem, wrecv_sem,
 ):
     me = lax.axis_index("mp")
     my_dp = lax.axis_index("dp")
@@ -119,7 +119,7 @@
             y = b * (CHUNK // 128) + i
             rs[rows((y + 1) * 16, 16), :] = q[16:32] + right(q[0:16]) + left(q[32:48])
 
-    each(0, 16384 // CHUNK, unet_rows)
+    each(0, 16384 // CHUNK, unet_rows, 4)
 
     for o in range(4):
         nz[pl.ds(o, 8, stride=4), :] = nbuf[0, o]
@@ -162,7 +162,7 @@
     for k in range(9):
         ky, kx = divmod(k, 3)
         put = jnp.where(iota((48, 4), 0) == kx * 16 + ky * 4 + iota((48, 4), 1), 1.0, 0.0).astype(BF16)
-        w_rows = w_rows + dot_nt(put, wibuf[k])
+        w_rows = w_rows + dot(put, wibuf[k])
     w48[...] = w_rows.astype(BF16)
     for copy in loads[7:]:
         copy.wait()
@@ -199,7 +199,7 @@
         s1[rows(r * 128, 128), :] = sig + act * (1.0 - sig)
         spread(h3, r, act, 0, 2)
 
-    each(0, 10, hidden)
+    each(0, 10, hidden, 5)
 
     def mixed(b):
         acc = jnp.broadcast_to(bmbuf[...], (4 * 128, 512))
@@ -212,7 +212,7 @@
             sig = 0.5 * jnp.tanh(0.5 * pre) + 0.5
             spread(m3, b * 4 + i, hbuf[...] * (sig + (pre * sig) * (1.0 - sig)), 2, 0)
 
-    each(0, 8 // 4, mixed)
+    each(0, 8 // 4, mixed, 2)
 
     gacc[1024:1280, :] = jnp.zeros((256, 512), F32)
     for ky in range(3):
@@ -228,7 +228,7 @@
         at = pl.ds(4 * r, 16)
         lacc[at, :] = lacc[at, :] + (q[16:32] + left(q[0:16]) + right(q[32:48]))
 
-    each(0, 10, latent_rows)
+    each(0, 10, latent_rows, 10)
     ngblk[...] = (-ratio * lacc[0:48, :]).astype(BF16)
 
     def ng_copy(peer, slot):
@@ -262,7 +262,7 @@
         ns[2, at, :] = right(v)
         return c
 
-    lax.fori_loop(0, N, shift, 0)
+    lax.fori_loop(0, N, shift, 0, unroll=4)
 
     def columns(b, acc):
         parts = []
@@ -274,7 +274,7 @@
         im[:, at] = block
         return acc + dot_nt(f2[:, at], block)
 
-    wg = lax.fori_loop(0, 16384 // CHUNK, columns, jnp.zeros((32, 48), F32))
+    wg = lax.fori_loop(0, 16384 // CHUNK, columns, jnp.zeros((32, 48), F32), unroll=4)
     wg = jnp.concatenate([wg[0:24], jnp.zeros((24, 80), F32)], axis=1)
     lane = iota((24, 128), 1)
     ordered = jnp.zeros((24, 128), F32)
@@ -307,21 +307,17 @@
         for i in range(CHUNK // 128):
             stage[pl.ds(b * (CHUNK // 128) + i, 24, stride=STRIDE), :] = p[0:24, i * 128 : (i + 1) * 128]
 
-    each(0, 16384 // CHUNK, feature)
+    each(0, 16384 // CHUNK, feature, 4)
     for c in range(20):
-        fgb[0, c] = stage[c * STRIDE : c * STRIDE + 128, :].astype(BF16)
-    fg_store = pltpu.make_async_copy(fgb, fg_out, out_sem.at[0])
-    fg_store.start()
+        fg_out[0, c] = stage[c * STRIDE : c * STRIDE + 128, :].astype(BF16)
     each(1, N, wg_take)
     acc = wrecv[0]
     for s in range(1, N):
         acc = acc + wrecv[s]
     acc = acc * (1.0 / 16384.0)
-    wgb[0:8, :] = acc[:, 0:36]
-    wgb[8:16, :] = pltpu.roll(acc, 88, 1)[:, 0:36]
-    wgb[16:20, :] = pltpu.roll(acc, 48, 1)[0:4, 0:36]
-    wg_store = pltpu.make_async_copy(wgb, wg_out, out_sem.at[1])
-    wg_store.start()
+    wg_out[0:8, :] = acc[:, 0:36]
+    wg_out[8:16, :] = pltpu.roll(acc, 88, 1)[:, 0:36]
+    wg_out[16:20, :] = pltpu.roll(acc, 48, 1)[0:4, 0:36]
 
     def sent(j):
         lat_copy(lax.rem(me + j, N), j).wait_send()
@@ -329,8 +325,6 @@
         wg_copy(lax.rem(my_dp + j, N), my_dp).wait_send()
 
     each(1, N, sent)
-    fg_store.wait()
-    wg_store.wait()
 
 
 def body(features, w_out, noisy_latent, timestep, w_in, b_in, w_mid, b_mid, reward_head):
@@ -343,14 +337,14 @@
             jax.ShapeDtypeStruct((20, 36), F32),
         ),
         in_specs=[hbm] * 10,
-        out_specs=(hbm, hbm),
+        out_specs=(pl.BlockSpec(memory_space=pltpu.VMEM),) * 2,
         scratch_shapes=[
             pltpu.VMEM((1, 20, 128, 128), BF16),
             pltpu.VMEM((20, 36), BF16),
             pltpu.VMEM((1, 4, 8, 128), F32),
             pltpu.SMEM((1,), jnp.int32),
             pltpu.VMEM((8, 128), F32),
-            pltpu.VMEM((9, 512, 4), BF16),
+            pltpu.VMEM((9, 4, 512), BF16),
             pltpu.VMEM((1, 512), F32),
             pltpu.VMEM((9, 512, 512), BF16),
             pltpu.VMEM((1, 512), F32),
@@ -375,15 +369,13 @@
             pltpu.VMEM((N, 48, 128), BF16),
             pltpu.VMEM((3, 528, 128), F32),
             pltpu.VMEM((48, 16384), BF16),
-            pltpu.VMEM((1, 20, 128, 128), BF16),
-            pltpu.VMEM((20, 36), F32),
             pltpu.VMEM((N, 8, 128), F32),
-            dma((10,)), dma((2,)), dma((N,)), dma((N,)), dma((N,)), dma((N,)), dma((N,)), dma((N,)),
+            dma((10,)), dma((N,)), dma((N,)), dma((N,)), dma((N,)), dma((N,)), dma((N,)),
         ],
         compiler_params=pltpu.CompilerParams(collective_id=0, has_side_effects=True, vmem_limit_bytes=56 << 20),
         name="step",
     )(
-        features, w_out, noisy_latent, timestep, jnp.asarray(noise_table()), w_in,
+        features, w_out, noisy_latent, timestep, jnp.asarray(noise_table()), w_in.transpose(0, 2, 1),
         b_in.reshape(1, 512), w_mid, b_mid.reshape(1, 512), reward_head.reshape(1, 512),
     )
 

time: 57.2 us -> 46.1 us (0.81)
  Pallas kernels: 50.2 us -> 41.4 us
  local copies, waits for them, and re-layouts: 5.53 us -> 3.29 us
    pallas_call x1, Pallas kernels: 50.2 us -> 41.4 us  [body(): pl.pallas_call(kernel, out_shape=(jax.ShapeDtypeStruct((1, 20, 128, 128),...]
    unnamed x3 -> x2, local copies, waits for them, and re-layouts: 5.53 us -> 3.29 us
where the time goes in v1:
time: 46.1 us; the launch traced here: 46 us
  Pallas kernels  41.4 us (90%)
  local copies, waits for them, and re-layouts  3.29 us (7%)
  between operations  1.29 us (3%)
    pallas_call x1, Pallas kernels, body(): pl.pallas_call(kernel, out_shape=(jax.ShapeDtypeStruct((1, 20, 128, 128),...  41.4 us
    unnamed x2, local copies, waits for them, and re-layouts  3.29 us

profile of v1, /device:TPU:1, one launch (start us, length us, event | category | flops | bytes accessed | tf_op | source)
XLA Modules:
  0.0 46.0 jit_solution(15046841931330980437)
XLA Ops:
  1.3 41.4 %step.1 = (bf16[1,20,128,128]{3,2,1,0:T(8,128)(2,1)}, f32[20,36]{1,0:T(8,128)}) custom-call(bf16[1,20,128,128]{3,2,1,0:T(8,128)(2,1)} %feat.1, bf16[20,36]{1,0:T(8,128)(2,1)} %w_out.1, f32[1,4,8,128]{3,2,1,0:T(8,128)} %noisy.1, s32[1]{0:T(128)S(6)} %copy.14.tstep, f32[8,128]{1,0:T(8,128)} %constant.2.clone.table, bf16[9,4,512]{2,1,0:T(4,128)(2,1)} %bitcast.4, ...), custom_call_target="tpu_custom_call" | custom-call | tf_op jit(solution)/shard_map/step/pallas_call | solution.py:333
  42.7 2.0 %copy.15 = bf16[1,20,128,128]{3,2,1,0:T(8,128)(2,1)} copy(bf16[1,20,128,128]{3,2,1,0:T(8,128)(2,1)} %get-tuple-element.4) | data formatting | bytes 1310720
  44.7 1.3 %copy.16 = f32[20,36]{1,0:T(8,128)} copy(f32[20,36]{1,0:T(8,128)} %get-tuple-element.5) | data formatting | bytes 5760

commit v2 on v0

--- a/solution.py
+++ b/solution.py
@@ -15,6 +15,16 @@
 NT = (((1,), (1,)), ((), ()))
 
 
+MP_FAR = sorted(
+    ((z, y, c) for z in range(2) for y in range(4) for c in range(2) if z or y or c),
+    key=lambda d: -4 * (d[0] + min(d[1], 4 - d[1])) - d[2],
+)
+DP_FAR = sorted(
+    ((x, z) for x in range(4) for z in range(4) if x or z),
+    key=lambda d: -min(d[0], 4 - d[0]) - 2 * min(d[1], 4 - d[1]),
+)
+
+
 def noise_table():
     betas = np.linspace(0.00085**0.5, 0.012**0.5, 1000, dtype=np.float32) ** 2
     table = np.cumprod((1.0 - betas).astype(np.float32), dtype=np.float32)
@@ -45,12 +55,12 @@
     return pl.ds(pl.multiple_of(start, size), size)
 
 
-def each(lo, hi, step):
+def each(lo, hi, step, unroll=1):
     def run(j, c):
         step(j)
         return c
 
-    lax.fori_loop(lo, hi, run, 0)
+    lax.fori_loop(lo, hi, run, 0, unroll=unroll)
 
 
 def kernel(
@@ -65,8 +75,13 @@
     my_dp = lax.axis_index("dp")
     pairs = ((feat, fbuf), (w_out, wobuf), (noisy, nbuf), (tstep, tbuf), (table, tabbuf),
              (w_in, wibuf), (b_in, bibuf), (b_mid, bmbuf), (head, hbuf), (w_mid, wmbuf))
+    mp_peers = [
+        lax.rem(me // 8 + z, 2) * 8 + lax.rem(lax.rem(me // 2, 4) + y, 4) * 2 + lax.rem(lax.rem(me, 2) + c, 2)
+        for z, y, c in MP_FAR
+    ]
+    dp_peers = [lax.rem(my_dp // 4 + x, 4) * 4 + lax.rem(lax.rem(my_dp, 4) + z, 4) for x, z in DP_FAR]
     loads = [pltpu.make_async_copy(src, dst, in_sem.at[i]) for i, (src, dst) in enumerate(pairs)]
-    for copy in loads:
+    for copy in loads[:-1]:
         copy.start()
     barrier = pltpu.get_barrier_semaphore()
 
@@ -98,6 +113,7 @@
     e48[:, 0:20] = dot_nt(pick_t, wobuf[...])
 
     loads[0].wait()
+    loads[-1].start()
     for c in range(20):
         stage[c * STRIDE : c * STRIDE + 128, :] = fbuf[0, c].astype(F32)
     for c in range(20, 24):
@@ -119,7 +135,7 @@
             y = b * (CHUNK // 128) + i
             rs[rows((y + 1) * 16, 16), :] = q[16:32] + right(q[0:16]) + left(q[32:48])
 
-    each(0, 16384 // CHUNK, unet_rows)
+    each(0, 16384 // CHUNK, unet_rows, 4)
 
     for o in range(4):
         nz[pl.ds(o, 8, stride=4), :] = nbuf[0, o]
@@ -154,7 +170,8 @@
         )
 
     pl.semaphore_wait(barrier, 2 * (N - 1))
-    each(1, N, lambda j: lat_copy(lax.rem(me + j, N), j).start())
+    for j, peer in enumerate(mp_peers):
+        lat_copy(peer, j + 1).start()
 
     loads[5].wait()
     loads[6].wait()
@@ -162,7 +179,7 @@
     for k in range(9):
         ky, kx = divmod(k, 3)
         put = jnp.where(iota((48, 4), 0) == kx * 16 + ky * 4 + iota((48, 4), 1), 1.0, 0.0).astype(BF16)
-        w_rows = w_rows + dot_nt(put, wibuf[k])
+        w_rows = w_rows + dot(put, wibuf[k])
     w48[...] = w_rows.astype(BF16)
     for copy in loads[7:]:
         copy.wait()
@@ -199,7 +216,7 @@
         s1[rows(r * 128, 128), :] = sig + act * (1.0 - sig)
         spread(h3, r, act, 0, 2)
 
-    each(0, 10, hidden)
+    each(0, 10, hidden, 10)
 
     def mixed(b):
         acc = jnp.broadcast_to(bmbuf[...], (4 * 128, 512))
@@ -212,7 +229,7 @@
             sig = 0.5 * jnp.tanh(0.5 * pre) + 0.5
             spread(m3, b * 4 + i, hbuf[...] * (sig + (pre * sig) * (1.0 - sig)), 2, 0)
 
-    each(0, 8 // 4, mixed)
+    each(0, 8 // 4, mixed, 2)
 
     gacc[1024:1280, :] = jnp.zeros((256, 512), F32)
     for ky in range(3):
@@ -228,7 +245,7 @@
         at = pl.ds(4 * r, 16)
         lacc[at, :] = lacc[at, :] + (q[16:32] + left(q[0:16]) + right(q[32:48]))
 
-    each(0, 10, latent_rows)
+    each(0, 10, latent_rows, 10)
     ngblk[...] = (-ratio * lacc[0:48, :]).astype(BF16)
 
     def ng_copy(peer, slot):
@@ -245,7 +262,8 @@
         peer = lax.rem(me + j, N)
         ng_copy(peer, peer).wait_recv()
 
-    each(1, N, lambda j: ng_copy(lax.rem(me + j, N), me).start())
+    for peer in mp_peers:
+        ng_copy(peer, me).start()
     grecv[me] = ngblk[...]
     ns[:, 0:8, :] = jnp.zeros((3, 8, 128), F32)
     ns[:, 512:528, :] = jnp.zeros((3, 16, 128), F32)
@@ -262,7 +280,7 @@
         ns[2, at, :] = right(v)
         return c
 
-    lax.fori_loop(0, N, shift, 0)
+    lax.fori_loop(0, N, shift, 0, unroll=4)
 
     def columns(b, acc):
         parts = []
@@ -274,7 +292,7 @@
         im[:, at] = block
         return acc + dot_nt(f2[:, at], block)
 
-    wg = lax.fori_loop(0, 16384 // CHUNK, columns, jnp.zeros((32, 48), F32))
+    wg = lax.fori_loop(0, 16384 // CHUNK, columns, jnp.zeros((32, 48), F32), unroll=4)
     wg = jnp.concatenate([wg[0:24], jnp.zeros((24, 80), F32)], axis=1)
     lane = iota((24, 128), 1)
     ordered = jnp.zeros((24, 128), F32)
@@ -298,7 +316,8 @@
         peer = lax.rem(my_dp + j, N)
         wg_copy(peer, peer).wait_recv()
 
-    each(1, N, lambda j: wg_copy(lax.rem(my_dp + j, N), my_dp).start())
+    for peer in dp_peers:
+        wg_copy(peer, my_dp).start()
 
     e_cols = e48t[...].astype(BF16)
 
@@ -307,11 +326,16 @@
         for i in range(CHUNK // 128):
             stage[pl.ds(b * (CHUNK // 128) + i, 24, stride=STRIDE), :] = p[0:24, i * 128 : (i + 1) * 128]
 
-    each(0, 16384 // CHUNK, feature)
+    each(0, 16384 // CHUNK, feature, 16)
     for c in range(20):
         fgb[0, c] = stage[c * STRIDE : c * STRIDE + 128, :].astype(BF16)
     fg_store = pltpu.make_async_copy(fgb, fg_out, out_sem.at[0])
     fg_store.start()
+    def sent(j):
+        lat_copy(lax.rem(me + j, N), j).wait_send()
+        ng_copy(lax.rem(me + j, N), me).wait_send()
+
+    each(1, N, sent)
     each(1, N, wg_take)
     acc = wrecv[0]
     for s in range(1, N):
@@ -322,26 +346,29 @@
     wgb[16:20, :] = pltpu.roll(acc, 48, 1)[0:4, 0:36]
     wg_store = pltpu.make_async_copy(wgb, wg_out, out_sem.at[1])
     wg_store.start()
-
-    def sent(j):
-        lat_copy(lax.rem(me + j, N), j).wait_send()
-        ng_copy(lax.rem(me + j, N), me).wait_send()
-        wg_copy(lax.rem(my_dp + j, N), my_dp).wait_send()
-
-    each(1, N, sent)
+    each(1, N, lambda j: wg_copy(lax.rem(my_dp + j, N), my_dp).wait_send())
     fg_store.wait()
     wg_store.wait()
+
+
+def publish(fg, wg, fg_out, wg_out, sem):
+    copies = [pltpu.make_async_copy(wg, wg_out, sem.at[4])]
+    for i in range(4):
+        part = pl.ds(5 * i, 5)
+        copies.append(pltpu.make_async_copy(fg.at[0, part], fg_out.at[0, part], sem.at[i]))
+    for copy in copies:
+        copy.start()
+    for copy in copies:
+        copy.wait()
 
 
 def body(features, w_out, noisy_latent, timestep, w_in, b_in, w_mid, b_mid, reward_head):
     hbm = pl.BlockSpec(memory_space=pltpu.HBM)
     dma = pltpu.SemaphoreType.DMA
-    return pl.pallas_call(
+    shapes = (jax.ShapeDtypeStruct((1, 20, 128, 128), BF16), jax.ShapeDtypeStruct((20, 36), F32))
+    fg, wg = pl.pallas_call(
         kernel,
-        out_shape=(
-            jax.ShapeDtypeStruct((1, 20, 128, 128), BF16),
-            jax.ShapeDtypeStruct((20, 36), F32),
-        ),
+        out_shape=shapes,
         in_specs=[hbm] * 10,
         out_specs=(hbm, hbm),
         scratch_shapes=[
@@ -350,7 +377,7 @@
             pltpu.VMEM((1, 4, 8, 128), F32),
             pltpu.SMEM((1,), jnp.int32),
             pltpu.VMEM((8, 128), F32),
-            pltpu.VMEM((9, 512, 4), BF16),
+            pltpu.VMEM((9, 4, 512), BF16),
             pltpu.VMEM((1, 512), F32),
             pltpu.VMEM((9, 512, 512), BF16),
             pltpu.VMEM((1, 512), F32),
@@ -383,9 +410,18 @@
         compiler_params=pltpu.CompilerParams(collective_id=0, has_side_effects=True, vmem_limit_bytes=56 << 20),
         name="step",
     )(
-        features, w_out, noisy_latent, timestep, jnp.asarray(noise_table()), w_in,
+        features, w_out, noisy_latent, timestep, jnp.asarray(noise_table()), w_in.transpose(0, 2, 1),
         b_in.reshape(1, 512), w_mid, b_mid.reshape(1, 512), reward_head.reshape(1, 512),
     )
+    return pl.pallas_call(
+        publish,
+        out_shape=shapes,
+        in_specs=[hbm, hbm],
+        out_specs=(hbm, hbm),
+        scratch_shapes=[dma((5,))],
+        compiler_params=pltpu.CompilerParams(vmem_limit_bytes=56 << 20),
+        name="publish",
+    )(fg, wg)
 
 
 def solution(mesh):

time: 57.2 us -> 61.8 us (1.080)
  Pallas kernels: 50.2 us -> 60.4 us
  local copies, waits for them, and re-layouts: 5.53 us -> 0 us
    pallas_call x1 -> x2, Pallas kernels: 50.2 us -> 60.4 us  [the longest x1 39.1 us: body(): pl.pallas_call(kernel, out_shape=shapes, in_specs=[hbm] * 10, out_specs=(...]
    unnamed x3 -> x0, local copies, waits for them, and re-layouts: 5.53 us -> none
where the time goes in v2:
time: 61.8 us; the launch traced here: 61.7 us
  Pallas kernels  60.4 us (98%)
  between operations  1.29 us (2%)
    pallas_call x1, Pallas kernels, body(): pl.pallas_call(kernel, out_shape=shapes, in_specs=[hbm] * 10, out_specs=(...  39.1 us
    pallas_call x1, Pallas kernels, body(): pl.pallas_call(publish, out_shape=shapes, in_specs=[hbm, hbm], out_specs=...  21.3 us

profile of v2, /device:TPU:1, one launch (start us, length us, event | category | flops | bytes accessed | tf_op | source)
XLA Modules:
  0.0 61.7 jit_solution(9805786851021142481)
XLA Ops:
  1.3 39.1 %step.1 = (bf16[1,20,128,128]{3,2,1,0:T(8,128)(2,1)}, f32[20,36]{1,0:T(8,128)}) custom-call(bf16[1,20,128,128]{3,2,1,0:T(8,128)(2,1)} %feat.1, bf16[20,36]{1,0:T(8,128)(2,1)} %w_out.1, f32[1,4,8,128]{3,2,1,0:T(8,128)} %noisy.1, s32[1]{0:T(128)S(6)} %copy.12.tstep, f32[8,128]{1,0:T(8,128)} %constant.2.clone.table, bf16[9,4,512]{2,1,0:T(4,128)(2,1)} %bitcast.4, ...), custom_call_target="tpu_custom_call" | custom-call | tf_op jit(solution)/shard_map/step/pallas_call | solution.py:369
  40.4 21.3 %publish.1 = (bf16[1,20,128,128]{3,2,1,0:T(8,128)(2,1)}, f32[20,36]{1,0:T(8,128)}) custom-call(bf16[1,20,128,128]{3,2,1,0:T(8,128)(2,1)} %get-tuple-element.4.fg, f32[20,36]{1,0:T(8,128)} %get-tuple-element.5.wg), custom_call_target="tpu_custom_call" | custom-call | tf_op jit(solution)/shard_map/publish/pallas_call | solution.py:416

commit v3 on v2

--- a/solution.py
+++ b/solution.py
@@ -68,8 +68,8 @@
     fg_out, wg_out,
     fbuf, wobuf, nbuf, tbuf, tabbuf, wibuf, bibuf, wmbuf, bmbuf, hbuf,
     stage, f2, rs, eacc, nz, eloc, recv, e48, e48t, w48, ls,
-    h3, s1, m3, gacc, lacc, ngblk, grecv, ns, im, fgb, wgb, wrecv,
-    in_sem, out_sem, send_sem, recv_sem, gsend_sem, grecv_sem, wsend_sem, wrecv_sem,
+    h3, s1, m3, gacc, lacc, ngblk, grecv, ns, im, wrecv,
+    in_sem, send_sem, recv_sem, gsend_sem, grecv_sem, wsend_sem, wrecv_sem,
 ):
     me = lax.axis_index("mp")
     my_dp = lax.axis_index("dp")
@@ -328,9 +328,7 @@
 
     each(0, 16384 // CHUNK, feature, 16)
     for c in range(20):
-        fgb[0, c] = stage[c * STRIDE : c * STRIDE + 128, :].astype(BF16)
-    fg_store = pltpu.make_async_copy(fgb, fg_out, out_sem.at[0])
-    fg_store.start()
+        fg_out[0, c] = stage[c * STRIDE : c * STRIDE + 128, :].astype(BF16)
     def sent(j):
         lat_copy(lax.rem(me + j, N), j).wait_send()
         ng_copy(lax.rem(me + j, N), me).wait_send()
@@ -341,21 +339,14 @@
     for s in range(1, N):
         acc = acc + wrecv[s]
     acc = acc * (1.0 / 16384.0)
-    wgb[0:8, :] = acc[:, 0:36]
-    wgb[8:16, :] = pltpu.roll(acc, 88, 1)[:, 0:36]
-    wgb[16:20, :] = pltpu.roll(acc, 48, 1)[0:4, 0:36]
-    wg_store = pltpu.make_async_copy(wgb, wg_out, out_sem.at[1])
-    wg_store.start()
+    wg_out[0:8, :] = acc[:, 0:36]
+    wg_out[8:16, :] = pltpu.roll(acc, 88, 1)[:, 0:36]
+    wg_out[16:20, :] = pltpu.roll(acc, 48, 1)[0:4, 0:36]
     each(1, N, lambda j: wg_copy(lax.rem(my_dp + j, N), my_dp).wait_send())
-    fg_store.wait()
-    wg_store.wait()
 
 
 def publish(fg, wg, fg_out, wg_out, sem):
-    copies = [pltpu.make_async_copy(wg, wg_out, sem.at[4])]
-    for i in range(4):
-        part = pl.ds(5 * i, 5)
-        copies.append(pltpu.make_async_copy(fg.at[0, part], fg_out.at[0, part], sem.at[i]))
+    copies = [pltpu.make_async_copy(fg, fg_out, sem.at[0]), pltpu.make_async_copy(wg, wg_out, sem.at[1])]
     for copy in copies:
         copy.start()
     for copy in copies:
@@ -364,13 +355,14 @@
 
 def body(features, w_out, noisy_latent, timestep, w_in, b_in, w_mid, b_mid, reward_head):
     hbm = pl.BlockSpec(memory_space=pltpu.HBM)
+    vmem = pl.BlockSpec(memory_space=pltpu.VMEM)
     dma = pltpu.SemaphoreType.DMA
     shapes = (jax.ShapeDtypeStruct((1, 20, 128, 128), BF16), jax.ShapeDtypeStruct((20, 36), F32))
     fg, wg = pl.pallas_call(
         kernel,
-        out_shape=shapes,
+        out_shape=(pltpu.VMEM(shapes[0].shape, BF16), pltpu.VMEM(shapes[1].shape, F32)),
         in_specs=[hbm] * 10,
-        out_specs=(hbm, hbm),
+        out_specs=(vmem, vmem),
         scratch_shapes=[
             pltpu.VMEM((1, 20, 128, 128), BF16),
             pltpu.VMEM((20, 36), BF16),
@@ -402,10 +394,8 @@
             pltpu.VMEM((N, 48, 128), BF16),
             pltpu.VMEM((3, 528, 128), F32),
             pltpu.VMEM((48, 16384), BF16),
-            pltpu.VMEM((1, 20, 128, 128), BF16),
-            pltpu.VMEM((20, 36), F32),
             pltpu.VMEM((N, 8, 128), F32),
-            dma((10,)), dma((2,)), dma((N,)), dma((N,)), dma((N,)), dma((N,)), dma((N,)), dma((N,)),
+            dma((10,)), dma((N,)), dma((N,)), dma((N,)), dma((N,)), dma((N,)), dma((N,)),
         ],
         compiler_params=pltpu.CompilerParams(collective_id=0, has_side_effects=True, vmem_limit_bytes=56 << 20),
         name="step",
@@ -416,10 +406,10 @@
     return pl.pallas_call(
         publish,
         out_shape=shapes,
-        in_specs=[hbm, hbm],
+        in_specs=[vmem, vmem],
         out_specs=(hbm, hbm),
-        scratch_shapes=[dma((5,))],
-        compiler_params=pltpu.CompilerParams(vmem_limit_bytes=56 << 20),
+        scratch_shapes=[dma((2,))],
+        compiler_params=pltpu.CompilerParams(vmem_limit_bytes=1 << 20),
         name="publish",
     )(fg, wg)
 

time: 61.8 us -> 40.9 us (0.66)
  Pallas kernels: 60.4 us -> 39.4 us
    pallas_call x2, Pallas kernels: 60.4 us -> 39.4 us  [the longest x1 38.6 us: body(): pl.pallas_call(kernel, out_shape=(pltpu.VMEM(shapes[0].shape, BF16), pltp...]
where the time goes in v3:
time: 40.9 us; the launch traced here: 40.7 us
  Pallas kernels  39.4 us (96%)
  between operations  1.29 us (3%)
    pallas_call x1, Pallas kernels, body(): pl.pallas_call(kernel, out_shape=(pltpu.VMEM(shapes[0].shape, BF16), pltp...  38.6 us
    pallas_call x1, Pallas kernels, body(): pl.pallas_call(publish, out_shape=shapes, in_specs=[vmem, vmem], out_spec...  0.86 us

profile of v3, /device:TPU:1, one launch (start us, length us, event | category | flops | bytes accessed | tf_op | source)
XLA Modules:
  0.0 40.7 jit_solution(6392565259909519038)
XLA Ops:
  1.3 38.6 %step.1 = (bf16[1,20,128,128]{3,2,1,0:T(8,128)(2,1)S(1)}, f32[20,36]{1,0:T(8,128)S(1)}) custom-call(bf16[1,20,128,128]{3,2,1,0:T(8,128)(2,1)} %feat.1, bf16[20,36]{1,0:T(8,128)(2,1)} %w_out.1, f32[1,4,8,128]{3,2,1,0:T(8,128)} %noisy.1, s32[1]{0:T(128)S(6)} %copy.12.tstep, f32[8,128]{1,0:T(8,128)} %constant.2.clone.table, bf16[9,4,512]{2,1,0:T(4,128)(2,1)} %bitcast.4, ...), custom_call_target="tpu_custom_call" | custom-call | tf_op jit(solution)/shard_map/step/pallas_call | solution.py:361
  39.9 0.9 %publish.1 = (bf16[1,20,128,128]{3,2,1,0:T(8,128)(2,1)}, f32[20,36]{1,0:T(8,128)}) custom-call(bf16[1,20,128,128]{3,2,1,0:T(8,128)(2,1)S(1)} %get-tuple-element.4.fg, f32[20,36]{1,0:T(8,128)S(1)} %get-tuple-element.5.wg), custom_call_target="tpu_custom_call" | custom-call | tf_op jit(solution)/shard_map/publish/pallas_call | solution.py:406

commit v4 on v3

--- a/solution.py
+++ b/solution.py
@@ -68,7 +68,7 @@
     fg_out, wg_out,
     fbuf, wobuf, nbuf, tbuf, tabbuf, wibuf, bibuf, wmbuf, bmbuf, hbuf,
     stage, f2, rs, eacc, nz, eloc, recv, e48, e48t, w48, ls,
-    h3, s1, m3, gacc, lacc, ngblk, grecv, ns, im, wrecv,
+    plus, minus, t3, s1, x3, lacc, ngblk, grecv, ns, im, wrecv,
     in_sem, send_sem, recv_sem, gsend_sem, grecv_sem, wsend_sem, wrecv_sem,
 ):
     me = lax.axis_index("mp")
@@ -184,6 +184,16 @@
     for copy in loads[7:]:
         copy.wait()
 
+    def points(i):
+        kx = i // 8
+        at = pl.ds(pl.multiple_of(lax.rem(i, 8) * 64, 64), 64)
+        even = 0.5 * (wmbuf[kx, at, :].astype(F32) + wmbuf[6 + kx, at, :].astype(F32))
+        odd = 0.5 * wmbuf[3 + kx, at, :].astype(F32)
+        plus[kx, at, :] = (even + odd).astype(BF16)
+        minus[kx, at, :] = (even - odd).astype(BF16)
+
+    each(0, 24, points)
+
     total = eacc[pl.ds(pl.multiple_of(32 * me, 32), 48), :]
 
     def lat_take(j, acc):
@@ -199,53 +209,80 @@
     edge = iota((128, 512), 0)
     first, last = edge == 0, edge == 127
 
-    def spread(dst, r, val, down, up):
-        at = rows(r * 128, 128)
-        dst[at, down * 512 : down * 512 + 512] = jnp.where(first, 0.0, pltpu.roll(val, 1, 0)).astype(BF16)
-        dst[at, 512:1024] = val.astype(BF16)
-        dst[at, up * 512 : up * 512 + 512] = jnp.where(last, 0.0, pltpu.roll(val, 127, 0)).astype(BF16)
+    def spread(dst, q, p, val, down, up):
+        at = pl.ds(p * 128, 128)
+        dst[q, at, down * 512 : down * 512 + 512] = jnp.where(first, 0.0, pltpu.roll(val, 1, 0)).astype(BF16)
+        dst[q, at, 512:1024] = val.astype(BF16)
+        dst[q, at, up * 512 : up * 512 + 512] = jnp.where(last, 0.0, pltpu.roll(val, 127, 0)).astype(BF16)
 
     def hidden(r):
-        at = pl.ds(4 * r, 16)
+        at = slice(4 * r, 4 * r + 16)
         x48 = jnp.concatenate([ls[0, at, :], ls[1, at, :], ls[2, at, :]], axis=0)
         pre = dot(x48.T.astype(BF16), w48[...]) + bibuf[...]
         row = 8 * me - 1 + r
         half = jnp.where(jnp.logical_and(row >= 0, row < 128), 0.5, 0.0)
         sig = half * jnp.tanh(0.5 * pre) + half
         act = pre * sig
-        s1[rows(r * 128, 128), :] = sig + act * (1.0 - sig)
-        spread(h3, r, act, 0, 2)
-
-    each(0, 10, hidden, 10)
-
-    def mixed(b):
-        acc = jnp.broadcast_to(bmbuf[...], (4 * 128, 512))
-        for ky in range(3):
+        s1[r * 128 : (r + 1) * 128, :] = sig + act * (1.0 - sig)
+        return act
+
+    acts = {}
+    for p in range(4):
+        for r in range(2 * p, 2 * p + 4):
+            if r not in acts:
+                acts[r] = hidden(r)
+        d0, d1, d2, d3 = (acts[2 * p + i] for i in range(4))
+        for q, t in enumerate((d0 - d2, d1 + d2, d2 - d1, d1 - d3)):
+            spread(t3, q, p, t, 0, 2)
+
+    def mixed(g):
+        at = slice(g * 4 * 128, (g + 1) * 4 * 128)
+        prod = []
+        for q in range(4):
+            acc = None
             for kx in range(3):
-                a = h3[pl.ds(pl.multiple_of((b * 4 + ky) * 128, 128), 4 * 128), kx * 512 : kx * 512 + 512]
-                acc = acc + dot_nt(a, wmbuf[3 * ky + kx])
+                tap = (wmbuf.at[kx], plus.at[kx], minus.at[kx], wmbuf.at[6 + kx])[q]
+                d = dot_nt(t3[q, at, kx * 512 : kx * 512 + 512], tap[...])
+                acc = d if acc is None else acc + d
+            prod.append(acc)
         for i in range(4):
-            pre = acc[i * 128 : (i + 1) * 128]
-            sig = 0.5 * jnp.tanh(0.5 * pre) + 0.5
-            spread(m3, b * 4 + i, hbuf[...] * (sig + (pre * sig) * (1.0 - sig)), 2, 0)
-
-    each(0, 8 // 4, mixed, 2)
-
-    gacc[1024:1280, :] = jnp.zeros((256, 512), F32)
-    for ky in range(3):
-        g = dot(m3[...], wmbuf[3 * ky : 3 * ky + 3].reshape(1536, 512))
-        at = pl.ds(ky * 128, 1024)
-        gacc[at, :] = g if ky == 0 else gacc[at, :] + g
+            m0, m1, m2, m3 = (m[i * 128 : (i + 1) * 128] for m in prod)
+            m1 = m1 + bmbuf[...]
+            grads = []
+            for pre in (m0 + m1 + m2, m1 - m2 - m3):
+                sig = 0.5 * jnp.tanh(0.5 * pre) + 0.5
+                grads.append(hbuf[...] * (sig + (pre * sig) * (1.0 - sig)))
+            g0, g1 = grads
+            for q, x in enumerate((g0, g0 + g1, g0 - g1, g1)):
+                spread(x3, q, g * 4 + i, x, 2, 0)
+
+    for g in range(4 // 4):
+        mixed(g)
+
     lacc[...] = jnp.zeros((56, 128), F32)
 
-    def latent_rows(r):
-        at = rows(r * 128, 128)
-        g = (gacc[at, :] * s1[at, :]).astype(BF16)
+    def latent_rows(r, val):
+        g = (val * s1[r * 128 : (r + 1) * 128, :]).astype(BF16)
         q = dot_nt(w48[...], g)
-        at = pl.ds(4 * r, 16)
+        at = slice(4 * r, 4 * r + 16)
         lacc[at, :] = lacc[at, :] + (q[16:32] + left(q[0:16]) + right(q[32:48]))
 
-    each(0, 10, latent_rows, 10)
+    carry = None
+    for g in range(4 // 4):
+        at = slice(g * 4 * 128, (g + 1) * 4 * 128)
+        taps = (wmbuf.at[0:3], plus, minus, wmbuf.at[6:9])
+        prod = [dot(x3[q, at, :], taps[q][...].reshape(1536, 512)) for q in range(4)]
+        for i in range(4):
+            p0, p1, p2, p3 = (m[i * 128 : (i + 1) * 128] for m in prod)
+            c0, c1, c2, c3 = p0, p1 - p2 - p3, p1 + p2 - p0, p3
+            if carry is not None:
+                c0, c1 = c0 + carry[0], c1 + carry[1]
+            p = g * 4 + i
+            latent_rows(2 * p, c0)
+            latent_rows(2 * p + 1, c1)
+            carry = (c2, c3)
+    latent_rows(8, carry[0])
+    latent_rows(9, carry[1])
     ngblk[...] = (-ratio * lacc[0:48, :]).astype(BF16)
 
     def ng_copy(peer, slot):
@@ -385,10 +422,11 @@
             pltpu.VMEM((32, 48), F32),
             pltpu.VMEM((48, 512), BF16),
             pltpu.VMEM((3, 56, 128), F32),
-            pltpu.VMEM((10 * 128, 1536), BF16),
+            pltpu.VMEM((3, 512, 512), BF16),
+            pltpu.VMEM((3, 512, 512), BF16),
+            pltpu.VMEM((4, 512, 1536), BF16),
             pltpu.VMEM((10 * 128, 512), F32),
-            pltpu.VMEM((8 * 128, 1536), BF16),
-            pltpu.VMEM((10 * 128, 512), F32),
+            pltpu.VMEM((4, 512, 1536), BF16),
             pltpu.VMEM((56, 128), F32),
             pltpu.VMEM((48, 128), BF16),
             pltpu.VMEM((N, 48, 128), BF16),

time: 40.9 us -> 38.1 us (0.932)
  Pallas kernels: 39.4 us -> 36.6 us
    pallas_call x1, Pallas kernels: 38.6 us -> 35.8 us  [body(): pl.pallas_call(kernel, out_shape=(pltpu.VMEM(shapes[0].shape, BF16), pltp...]
where the time goes in v4:
time: 38.1 us; the launch traced here: 37.9 us
  Pallas kernels  36.6 us (96%)
  between operations  1.29 us (3%)
    pallas_call x1, Pallas kernels, body(): pl.pallas_call(kernel, out_shape=(pltpu.VMEM(shapes[0].shape, BF16), pltp...  35.8 us
    pallas_call x1, Pallas kernels, body(): pl.pallas_call(publish, out_shape=shapes, in_specs=[vmem, vmem], out_spec...  0.86 us

profile of v4, /device:TPU:1, one launch (start us, length us, event | category | flops | bytes accessed | tf_op | source)
XLA Modules:
  0.0 37.9 jit_solution(9458193709149079186)
XLA Ops:
  1.3 35.8 %step.1 = (bf16[1,20,128,128]{3,2,1,0:T(8,128)(2,1)S(1)}, f32[20,36]{1,0:T(8,128)S(1)}) custom-call(bf16[1,20,128,128]{3,2,1,0:T(8,128)(2,1)} %feat.1, bf16[20,36]{1,0:T(8,128)(2,1)} %w_out.1, f32[1,4,8,128]{3,2,1,0:T(8,128)} %noisy.1, s32[1]{0:T(128)S(6)} %copy.12.tstep, f32[8,128]{1,0:T(8,128)} %constant.2.clone.table, bf16[9,4,512]{2,1,0:T(4,128)(2,1)} %bitcast.4, ...), custom_call_target="tpu_custom_call" | custom-call | tf_op jit(solution)/shard_map/step/pallas_call | solution.py:398
  37.1 0.9 %publish.1 = (bf16[1,20,128,128]{3,2,1,0:T(8,128)(2,1)}, f32[20,36]{1,0:T(8,128)}) custom-call(bf16[1,20,128,128]{3,2,1,0:T(8,128)(2,1)S(1)} %get-tuple-element.4.fg, f32[20,36]{1,0:T(8,128)S(1)} %get-tuple-element.5.wg), custom_call_target="tpu_custom_call" | custom-call | tf_op jit(solution)/shard_map/publish/pallas_call | solution.py:444

commit v5 on v3

--- a/solution.py
+++ b/solution.py
@@ -25,6 +25,9 @@
 )
 
 
+SLOT = {q: i for i, q in enumerate((a, b) for a in range(4) for b in range(4) if a % 3 or b % 3)}
+
+
 def noise_table():
     betas = np.linspace(0.00085**0.5, 0.012**0.5, 1000, dtype=np.float32) ** 2
     table = np.cumprod((1.0 - betas).astype(np.float32), dtype=np.float32)
@@ -68,7 +71,7 @@
     fg_out, wg_out,
     fbuf, wobuf, nbuf, tbuf, tabbuf, wibuf, bibuf, wmbuf, bmbuf, hbuf,
     stage, f2, rs, eacc, nz, eloc, recv, e48, e48t, w48, ls,
-    h3, s1, m3, gacc, lacc, ngblk, grecv, ns, im, wrecv,
+    upts, t3, s1, x3, gbuf, mm, lacc, ngblk, grecv, ns, im, wrecv,
     in_sem, send_sem, recv_sem, gsend_sem, grecv_sem, wsend_sem, wrecv_sem,
 ):
     me = lax.axis_index("mp")
@@ -184,6 +187,27 @@
     for copy in loads[7:]:
         copy.wait()
 
+    def points(i):
+        at = pl.ds(pl.multiple_of(i * 16, 16), 16)
+        cols = []
+        for kx in range(3):
+            w0, w1, w2 = (wmbuf[3 * ky + kx, at, :].astype(F32) for ky in range(3))
+            even, odd = 0.5 * (w0 + w2), 0.5 * w1
+            cols.append((w0, even + odd, even - odd, w2))
+        for qy in range(4):
+            w0, w1, w2 = (col[qy] for col in cols)
+            even, odd = 0.5 * (w0 + w2), 0.5 * w1
+            for qx, u in enumerate((w0, even + odd, even - odd, w2)):
+                if (qy, qx) in SLOT:
+                    upts[SLOT[qy, qx], at, :] = u.astype(BF16)
+
+    each(0, 32, points, 4)
+
+    def taps(qy, qx, d, c):
+        if (qy, qx) in SLOT:
+            return upts[SLOT[qy, qx], d, c]
+        return wmbuf[2 * qy + 2 * qx // 3, d, c]
+
     total = eacc[pl.ds(pl.multiple_of(32 * me, 32), 48), :]
 
     def lat_take(j, acc):
@@ -192,61 +216,137 @@
 
     total = lax.fori_loop(1, N, lat_take, total)
 
-    lat = total.astype(BF16).astype(F32)
-    for i, t in enumerate((right(lat), lat, left(lat))):
+    def column(b):
+        return jnp.where(b < 64, 2 * b, 2 * b - 127)
+
+    to_halves = jnp.where(iota((128, 128), 0) == column(iota((128, 128), 1)), 1.0, 0.0).astype(BF16)
+    to_columns = jnp.where(iota((128, 128), 1) == column(iota((128, 128), 0)), 1.0, 0.0).astype(BF16)
+
+    def from_right(v):
+        lane = iota(v.shape, 1)
+        v = jnp.where(lane < 64, pltpu.roll(v, 64, 1), pltpu.roll(v, 63, 1))
+        return jnp.where(lane == 127, 0.0, v)
+
+    def from_left(v):
+        lane = iota(v.shape, 1)
+        v = jnp.where(lane < 64, pltpu.roll(v, 65, 1), pltpu.roll(v, 64, 1))
+        return jnp.where(lane == 0, 0.0, v)
+
+    lat = dot(total.astype(BF16), to_halves)
+    for i, t in enumerate((from_left(lat), lat, from_right(lat))):
         ls[i, 0:48, :] = t
         ls[i, 48:56, :] = jnp.zeros((8, 128), F32)
-    edge = iota((128, 512), 0)
-    first, last = edge == 0, edge == 127
-
-    def spread(dst, r, val, down, up):
-        at = rows(r * 128, 128)
-        dst[at, down * 512 : down * 512 + 512] = jnp.where(first, 0.0, pltpu.roll(val, 1, 0)).astype(BF16)
-        dst[at, 512:1024] = val.astype(BF16)
-        dst[at, up * 512 : up * 512 + 512] = jnp.where(last, 0.0, pltpu.roll(val, 127, 0)).astype(BF16)
+
+    def down(v):
+        return jnp.where(iota(v.shape, 0) == 0, 0.0, pltpu.roll(v, 1, 0))
+
+    def up(v):
+        return jnp.where(iota(v.shape, 0) == 63, 0.0, pltpu.roll(v, 63, 0))
+
+    def combine(m0, m1, m2, m3):
+        return m0 + m1 + m2, m1 - m2 - m3
+
+    def scatter(p0, p1, p2, p3):
+        return p0, p1 - p2 - p3, p1 + p2 - p0, p3
 
     def hidden(r):
-        at = pl.ds(4 * r, 16)
+        at = slice(4 * r, 4 * r + 16)
         x48 = jnp.concatenate([ls[0, at, :], ls[1, at, :], ls[2, at, :]], axis=0)
         pre = dot(x48.T.astype(BF16), w48[...]) + bibuf[...]
         row = 8 * me - 1 + r
         half = jnp.where(jnp.logical_and(row >= 0, row < 128), 0.5, 0.0)
         sig = half * jnp.tanh(0.5 * pre) + half
         act = pre * sig
-        s1[rows(r * 128, 128), :] = sig + act * (1.0 - sig)
-        spread(h3, r, act, 0, 2)
-
-    each(0, 10, hidden, 10)
-
-    def mixed(b):
-        acc = jnp.broadcast_to(bmbuf[...], (4 * 128, 512))
-        for ky in range(3):
-            for kx in range(3):
-                a = h3[pl.ds(pl.multiple_of((b * 4 + ky) * 128, 128), 4 * 128), kx * 512 : kx * 512 + 512]
-                acc = acc + dot_nt(a, wmbuf[3 * ky + kx])
-        for i in range(4):
-            pre = acc[i * 128 : (i + 1) * 128]
-            sig = 0.5 * jnp.tanh(0.5 * pre) + 0.5
-            spread(m3, b * 4 + i, hbuf[...] * (sig + (pre * sig) * (1.0 - sig)), 2, 0)
-
-    each(0, 8 // 4, mixed, 2)
-
-    gacc[1024:1280, :] = jnp.zeros((256, 512), F32)
-    for ky in range(3):
-        g = dot(m3[...], wmbuf[3 * ky : 3 * ky + 3].reshape(1536, 512))
-        at = pl.ds(ky * 128, 1024)
-        gacc[at, :] = g if ky == 0 else gacc[at, :] + g
+        s1[r * 128 : (r + 1) * 128, :] = sig + act * (1.0 - sig)
+        return act
+
+    acts = {}
+    for p in range(4):
+        for r in range(2 * p, 2 * p + 4):
+            if r not in acts:
+                acts[r] = hidden(r)
+        d0, d1, d2, d3 = (acts[2 * p + i] for i in range(4))
+        for qy, t in enumerate((d0 - d2, d1 + d2, d2 - d1, d1 - d3)):
+            even, odd = t[0:64], t[64:128]
+            for qx, u in enumerate((down(odd) - odd, even + odd, odd - even, even - up(even))):
+                t3[4 * qy + qx, p * 64 : p * 64 + 64, :] = u.astype(BF16)
+
+    HALF = 512 // 2
+
+    def channels(n):
+        return slice(n * HALF, (n + 1) * HALF)
+
+    def forward(n, qy):
+        for qx in range(4):
+            mm[n % 2, 4 * qy + qx] = dot_nt(t3[4 * qy + qx], taps(qy, qx, channels(n), slice(None)))
+
+    def mixed(n, p):
+        at, ch = slice(p * 64, p * 64 + 64), channels(n)
+        grads = []
+        sums = [combine(*(mm[n % 2, 4 * qy + qx, at, :] for qx in range(4))) for qy in range(4)]
+        for side in range(2):
+            m0, m1, m2, m3 = (pair[side] for pair in sums)
+            out = []
+            for pre in combine(m0, m1 + bmbuf[:, ch], m2, m3):
+                sig = 0.5 * jnp.tanh(0.5 * pre) + 0.5
+                out.append(hbuf[:, ch] * (sig + (pre * sig) * (1.0 - sig)))
+            g0, g1 = out
+            grads.append((g0, g0 + g1, g0 - g1, g1))
+        for qy in range(4):
+            even, odd = grads[0][qy], grads[1][qy]
+            for qx, u in enumerate((even, even + odd, even - odd, odd)):
+                x3[4 * qy + qx, at, ch] = u.astype(BF16)
+
+    for n in range(2):
+        for qy in range(4):
+            forward(n, qy)
+            if n > 0:
+                mixed(n - 1, qy)
+    for p in range(4):
+        mixed(2 - 1, p)
+
     lacc[...] = jnp.zeros((56, 128), F32)
 
-    def latent_rows(r):
-        at = rows(r * 128, 128)
-        g = (gacc[at, :] * s1[at, :]).astype(BF16)
-        q = dot_nt(w48[...], g)
-        at = pl.ds(4 * r, 16)
-        lacc[at, :] = lacc[at, :] + (q[16:32] + left(q[0:16]) + right(q[32:48]))
-
-    each(0, 10, latent_rows, 10)
-    ngblk[...] = (-ratio * lacc[0:48, :]).astype(BF16)
+    def latent_rows(n, r, val):
+        at, ch = slice(r * 128, (r + 1) * 128), channels(n)
+        gbuf[at, ch] = (val * s1[at, ch]).astype(BF16)
+
+    def finish(n, r, p0, p1, p2, p3):
+        c0, c1, c2, c3 = scatter(p0, p1, p2, p3)
+        latent_rows(n, r, jnp.concatenate([c1 + down(c3), c2 + up(c0)], axis=0))
+
+    def backward(n, qy):
+        for qx in range(4):
+            mm[n % 2, 4 * qy + qx] = dot(x3[4 * qy + qx], taps(qy, qx, slice(None), channels(n)))
+
+    def give(n, p, carry):
+        at = slice(p * 64, p * 64 + 64)
+        given = [scatter(*(mm[n % 2, 4 * qy + qx, at, :] for qy in range(4))) for qx in range(4)]
+        if carry is not None:
+            given = [(g[0] + c[0], g[1] + c[1], g[2], g[3]) for g, c in zip(given, carry)]
+        finish(n, 2 * p, *(g[0] for g in given))
+        finish(n, 2 * p + 1, *(g[1] for g in given))
+        carry = [(g[2], g[3]) for g in given]
+        if p == 3:
+            finish(n, 8, *(c[0] for c in carry))
+            finish(n, 9, *(c[1] for c in carry))
+        return carry
+
+    carry = None
+    for n in range(2):
+        for qy in range(4):
+            backward(n, qy)
+            if n > 0:
+                carry = give(n - 1, qy, carry)
+        carry = None
+    for p in range(4):
+        carry = give(2 - 1, p, carry)
+    lat_parts = dot_nt(w48[...], gbuf[...])
+    for r in range(10):
+        q = lat_parts[:, r * 128 : (r + 1) * 128]
+        at = slice(4 * r, 4 * r + 16)
+        lacc[at, :] = lacc[at, :] + (q[16:32] + from_right(q[0:16]) + from_left(q[32:48]))
+    ngblk[...] = dot((-ratio * lacc[0:48, :]).astype(BF16), to_columns).astype(BF16)
 
     def ng_copy(peer, slot):
         return pltpu.make_async_remote_copy(
@@ -280,7 +380,7 @@
         ns[2, at, :] = right(v)
         return c
 
-    lax.fori_loop(0, N, shift, 0, unroll=4)
+    lax.fori_loop(0, N, shift, 0, unroll=16)
 
     def columns(b, acc):
         parts = []
@@ -292,7 +392,7 @@
         im[:, at] = block
         return acc + dot_nt(f2[:, at], block)
 
-    wg = lax.fori_loop(0, 16384 // CHUNK, columns, jnp.zeros((32, 48), F32), unroll=4)
+    wg = lax.fori_loop(0, 16384 // CHUNK, columns, jnp.zeros((32, 48), F32), unroll=8)
     wg = jnp.concatenate([wg[0:24], jnp.zeros((24, 80), F32)], axis=1)
     lane = iota((24, 128), 1)
     ordered = jnp.zeros((24, 128), F32)
@@ -385,10 +485,12 @@
             pltpu.VMEM((32, 48), F32),
             pltpu.VMEM((48, 512), BF16),
             pltpu.VMEM((3, 56, 128), F32),
-            pltpu.VMEM((10 * 128, 1536), BF16),
+            pltpu.VMEM((12, 512, 512), BF16),
+            pltpu.VMEM((16, 256, 512), BF16),
             pltpu.VMEM((10 * 128, 512), F32),
-            pltpu.VMEM((8 * 128, 1536), BF16),
-            pltpu.VMEM((10 * 128, 512), F32),
+            pltpu.VMEM((16, 256, 512), BF16),
+            pltpu.VMEM((10 * 128, 512), BF16),
+            pltpu.VMEM((2, 16, 256, 512 // 2), F32),
             pltpu.VMEM((56, 128), F32),
             pltpu.VMEM((48, 128), BF16),
             pltpu.VMEM((N, 48, 128), BF16),

time: 40.9 us -> 37 us (0.905)
  Pallas kernels: 39.4 us -> 35.5 us
    pallas_call x1, Pallas kernels: 38.6 us -> 34.7 us  [body(): pl.pallas_call(kernel, out_shape=(pltpu.VMEM(shapes[0].shape, BF16), pltp...]
where the time goes in v5:
time: 37 us; the launch traced here: 36.8 us
  Pallas kernels  35.5 us (96%)
  between operations  1.29 us (3%)
    pallas_call x1, Pallas kernels, body(): pl.pallas_call(kernel, out_shape=(pltpu.VMEM(shapes[0].shape, BF16), pltp...  34.7 us
    pallas_call x1, Pallas kernels, body(): pl.pallas_call(publish, out_shape=shapes, in_specs=[vmem, vmem], out_spec...  0.86 us

profile of v5, /device:TPU:1, one launch (start us, length us, event | category | flops | bytes accessed | tf_op | source)
XLA Modules:
  0.0 36.8 jit_solution(17864594795395522558)
XLA Ops:
  1.3 34.7 %step.1 = (bf16[1,20,128,128]{3,2,1,0:T(8,128)(2,1)S(1)}, f32[20,36]{1,0:T(8,128)S(1)}) custom-call(bf16[1,20,128,128]{3,2,1,0:T(8,128)(2,1)} %feat.1, bf16[20,36]{1,0:T(8,128)(2,1)} %w_out.1, f32[1,4,8,128]{3,2,1,0:T(8,128)} %noisy.1, s32[1]{0:T(128)S(6)} %copy.12.tstep, f32[8,128]{1,0:T(8,128)} %constant.2.clone.table, bf16[9,4,512]{2,1,0:T(4,128)(2,1)} %bitcast.4, ...), custom_call_target="tpu_custom_call" | custom-call | tf_op jit(solution)/shard_map/step/pallas_call | solution.py:461
  36.0 0.9 %publish.1 = (bf16[1,20,128,128]{3,2,1,0:T(8,128)(2,1)}, f32[20,36]{1,0:T(8,128)}) custom-call(bf16[1,20,128,128]{3,2,1,0:T(8,128)(2,1)S(1)} %get-tuple-element.4.fg, f32[20,36]{1,0:T(8,128)S(1)} %get-tuple-element.5.wg), custom_call_target="tpu_custom_call" | custom-call | tf_op jit(solution)/shard_map/publish/pallas_call | solution.py:508

commit v6 on v5

--- a/solution.py
+++ b/solution.py
@@ -54,8 +54,8 @@
     return jnp.where(iota(v.shape, 1) == 127, 0.0, pltpu.roll(v, 127, 1))
 
 
-def rows(start, size):
-    return pl.ds(pl.multiple_of(start, size), size)
+def rows(start, multiple, size=None):
+    return pl.ds(pl.multiple_of(start, multiple), size or multiple)
 
 
 def each(lo, hi, step, unroll=1):
@@ -211,8 +211,8 @@
     total = eacc[pl.ds(pl.multiple_of(32 * me, 32), 48), :]
 
     def lat_take(j, acc):
-        lat_copy(lax.rem(me + j, N), j).wait_recv()
-        return acc + recv[j].astype(F32)
+        lat_copy(lax.rem(me + j, N), N - j).wait_recv()
+        return acc + recv[N - j].astype(F32)
 
     total = lax.fori_loop(1, N, lat_take, total)
 
@@ -358,34 +358,28 @@
             device_id_type=MESH,
         )
 
-    def ng_take(j):
-        peer = lax.rem(me + j, N)
-        ng_copy(peer, peer).wait_recv()
+    def add_rows(peer):
+        at = rows(32 * peer, 16, 48)
+        v = grecv[peer].astype(F32)
+        ns[0, at, :] = ns[0, at, :] + left(v)
+        ns[1, at, :] = ns[1, at, :] + v
+        ns[2, at, :] = ns[2, at, :] + right(v)
 
     for peer in mp_peers:
         ng_copy(peer, me).start()
     grecv[me] = ngblk[...]
+    ns[...] = jnp.zeros((3, 528, 128), F32)
+    add_rows(me)
+    for peer in reversed(mp_peers):
+        ng_copy(peer, peer).wait_recv()
+        add_rows(peer)
     ns[:, 0:8, :] = jnp.zeros((3, 8, 128), F32)
-    ns[:, 512:528, :] = jnp.zeros((3, 16, 128), F32)
-    each(1, N, ng_take)
-
-    def shift(s, c):
-        at = pl.ds(4 + 32 * s, 32)
-        v = grecv[s].astype(F32)
-        above = jnp.where(s > 0, grecv[jnp.maximum(s - 1, 0), 40 - 8 : 48].astype(F32)[8:16], 0.0)
-        below = jnp.where(s < N - 1, grecv[jnp.minimum(s + 1, N - 1), 0:16].astype(F32)[0:8], 0.0)
-        v = jnp.concatenate([v[8:16] + above, v[16:32], v[32:40] + below], axis=0)
-        ns[0, at, :] = left(v)
-        ns[1, at, :] = v
-        ns[2, at, :] = right(v)
-        return c
-
-    lax.fori_loop(0, N, shift, 0, unroll=16)
+    ns[:, 520:528, :] = jnp.zeros((3, 8, 128), F32)
 
     def columns(b, acc):
         parts = []
         for i in range(CHUNK // 128):
-            at = pl.ds(4 * (b * (CHUNK // 128) + i), 16)
+            at = pl.ds(4 * (b * (CHUNK // 128) + i) + 4, 16)
             parts.append(jnp.concatenate([ns[k, at, :].astype(BF16) for k in range(3)], axis=0))
         block = jnp.concatenate(parts, axis=1)
         at = rows(b * CHUNK, CHUNK)

time: 37 us -> 37.2 us (level)
  no operation moved by 1% of the time
where the time goes in v6:
time: 37.2 us; the launch traced here: 37.1 us
  Pallas kernels  35.8 us (96%)
  between operations  1.29 us (3%)
    pallas_call x1, Pallas kernels, body(): pl.pallas_call(kernel, out_shape=(pltpu.VMEM(shapes[0].shape, BF16), pltp...  34.9 us
    pallas_call x1, Pallas kernels, body(): pl.pallas_call(publish, out_shape=shapes, in_specs=[vmem, vmem], out_spec...  0.86 us

profile of v6, /device:TPU:1, one launch (start us, length us, event | category | flops | bytes accessed | tf_op | source)
XLA Modules:
  0.0 37.1 jit_solution(1350926891779475293)
XLA Ops:
  1.3 34.9 %step.1 = (bf16[1,20,128,128]{3,2,1,0:T(8,128)(2,1)S(1)}, f32[20,36]{1,0:T(8,128)S(1)}) custom-call(bf16[1,20,128,128]{3,2,1,0:T(8,128)(2,1)} %feat.1, bf16[20,36]{1,0:T(8,128)(2,1)} %w_out.1, f32[1,4,8,128]{3,2,1,0:T(8,128)} %noisy.1, s32[1]{0:T(128)S(6)} %copy.12.tstep, f32[8,128]{1,0:T(8,128)} %constant.2.clone.table, bf16[9,4,512]{2,1,0:T(4,128)(2,1)} %bitcast.4, ...), custom_call_target="tpu_custom_call" | custom-call | tf_op jit(solution)/shard_map/step/pallas_call | solution.py:455
  36.2 0.9 %publish.1 = (bf16[1,20,128,128]{3,2,1,0:T(8,128)(2,1)}, f32[20,36]{1,0:T(8,128)}) custom-call(bf16[1,20,128,128]{3,2,1,0:T(8,128)(2,1)S(1)} %get-tuple-element.4.fg, f32[20,36]{1,0:T(8,128)S(1)} %get-tuple-element.5.wg), custom_call_target="tpu_custom_call" | custom-call | tf_op jit(solution)/shard_map/publish/pallas_call | solution.py:502

commit v7 on v5

--- a/solution.py
+++ b/solution.py
@@ -400,7 +400,8 @@
         ky, kx = divmod(k, 3)
         moved = pltpu.roll(wg, (4 * k - kx * 16 - (2 - ky) * 4) % 128, 1)
         ordered = jnp.where(jnp.logical_and(lane >= 4 * k, lane < 4 * k + 4), moved, ordered)
-    wrecv[my_dp] = ordered[0:8] + pltpu.roll(ordered[8:16], 40, 1) + pltpu.roll(ordered[16:24], 80, 1)
+    packed = ordered[0:8] + pltpu.roll(ordered[8:16], 40, 1) + pltpu.roll(ordered[16:24], 80, 1)
+    wrecv[my_dp] = packed.astype(BF16)
 
     def wg_copy(peer, slot):
         return pltpu.make_async_remote_copy(
@@ -432,17 +433,17 @@
     def sent(j):
         lat_copy(lax.rem(me + j, N), j).wait_send()
         ng_copy(lax.rem(me + j, N), me).wait_send()
+        wg_copy(lax.rem(my_dp + j, N), my_dp).wait_send()
 
     each(1, N, sent)
     each(1, N, wg_take)
-    acc = wrecv[0]
+    acc = wrecv[0].astype(F32)
     for s in range(1, N):
-        acc = acc + wrecv[s]
+        acc = acc + wrecv[s].astype(F32)
     acc = acc * (1.0 / 16384.0)
     wg_out[0:8, :] = acc[:, 0:36]
     wg_out[8:16, :] = pltpu.roll(acc, 88, 1)[:, 0:36]
     wg_out[16:20, :] = pltpu.roll(acc, 48, 1)[0:4, 0:36]
-    each(1, N, lambda j: wg_copy(lax.rem(my_dp + j, N), my_dp).wait_send())
 
 
 def publish(fg, wg, fg_out, wg_out, sem):
@@ -496,7 +497,7 @@
             pltpu.VMEM((N, 48, 128), BF16),
             pltpu.VMEM((3, 528, 128), F32),
             pltpu.VMEM((48, 16384), BF16),
-            pltpu.VMEM((N, 8, 128), F32),
+            pltpu.VMEM((N, 8, 128), BF16),
             dma((10,)), dma((N,)), dma((N,)), dma((N,)), dma((N,)), dma((N,)), dma((N,)),
         ],
         compiler_params=pltpu.CompilerParams(collective_id=0, has_side_effects=True, vmem_limit_bytes=56 << 20),

time: 37 us -> 36.8 us (level)
  no operation moved by 1% of the time
where the time goes in v7:
time: 36.8 us; the launch traced here: 36.7 us
  Pallas kernels  35.4 us (96%)
  between operations  1.29 us (4%)
    pallas_call x1, Pallas kernels, body(): pl.pallas_call(kernel, out_shape=(pltpu.VMEM(shapes[0].shape, BF16), pltp...  34.5 us
    pallas_call x1, Pallas kernels, body(): pl.pallas_call(publish, out_shape=shapes, in_specs=[vmem, vmem], out_spec...  0.86 us

profile of v7, /device:TPU:1, one launch (start us, length us, event | category | flops | bytes accessed | tf_op | source)
XLA Modules:
  0.0 36.7 jit_solution(4226915669313404100)
XLA Ops:
  1.3 34.5 %step.1 = (bf16[1,20,128,128]{3,2,1,0:T(8,128)(2,1)S(1)}, f32[20,36]{1,0:T(8,128)S(1)}) custom-call(bf16[1,20,128,128]{3,2,1,0:T(8,128)(2,1)} %feat.1, bf16[20,36]{1,0:T(8,128)(2,1)} %w_out.1, f32[1,4,8,128]{3,2,1,0:T(8,128)} %noisy.1, s32[1]{0:T(128)S(6)} %copy.12.tstep, f32[8,128]{1,0:T(8,128)} %constant.2.clone.table, bf16[9,4,512]{2,1,0:T(4,128)(2,1)} %bitcast.4, ...), custom_call_target="tpu_custom_call" | custom-call | tf_op jit(solution)/shard_map/step/pallas_call | solution.py:462
  35.8 0.9 %publish.1 = (bf16[1,20,128,128]{3,2,1,0:T(8,128)(2,1)}, f32[20,36]{1,0:T(8,128)}) custom-call(bf16[1,20,128,128]{3,2,1,0:T(8,128)(2,1)S(1)} %get-tuple-element.4.fg, f32[20,36]{1,0:T(8,128)S(1)} %get-tuple-element.5.wg), custom_call_target="tpu_custom_call" | custom-call | tf_op jit(solution)/shard_map/publish/pallas_call | solution.py:509

commit v8 on v5

--- a/solution.py
+++ b/solution.py
@@ -88,11 +88,10 @@
         copy.start()
     barrier = pltpu.get_barrier_semaphore()
 
-    def greet(j):
-        pl.semaphore_signal(barrier, inc=1, device_id={"mp": lax.rem(me + j, N)}, device_id_type=MESH)
-        pl.semaphore_signal(barrier, inc=1, device_id={"dp": lax.rem(my_dp + j, N)}, device_id_type=MESH)
-
-    each(1, N, greet)
+    for peer in dp_peers:
+        pl.semaphore_signal(barrier, inc=1, device_id={"dp": peer}, device_id_type=MESH)
+    for peer in mp_peers:
+        pl.semaphore_signal(barrier, inc=1, device_id={"mp": peer}, device_id_type=MESH)
 
     for copy in loads[1:5]:
         copy.wait()

time: 37 us -> 36.8 us (level)
  no operation moved by 1% of the time
where the time goes in v8:
time: 36.8 us; the launch traced here: 36.7 us
  Pallas kernels  35.4 us (96%)
  between operations  1.29 us (4%)
    pallas_call x1, Pallas kernels, body(): pl.pallas_call(kernel, out_shape=(pltpu.VMEM(shapes[0].shape, BF16), pltp...  34.6 us
    pallas_call x1, Pallas kernels, body(): pl.pallas_call(publish, out_shape=shapes, in_specs=[vmem, vmem], out_spec...  0.86 us

profile of v8, /device:TPU:1, one launch (start us, length us, event | category | flops | bytes accessed | tf_op | source)
XLA Modules:
  0.0 36.7 jit_solution(10048917881460939416)
XLA Ops:
  1.3 34.6 %step.1 = (bf16[1,20,128,128]{3,2,1,0:T(8,128)(2,1)S(1)}, f32[20,36]{1,0:T(8,128)S(1)}) custom-call(bf16[1,20,128,128]{3,2,1,0:T(8,128)(2,1)} %feat.1, bf16[20,36]{1,0:T(8,128)(2,1)} %w_out.1, f32[1,4,8,128]{3,2,1,0:T(8,128)} %noisy.1, s32[1]{0:T(128)S(6)} %copy.12.tstep, f32[8,128]{1,0:T(8,128)} %constant.2.clone.table, bf16[9,4,512]{2,1,0:T(4,128)(2,1)} %bitcast.4, ...), custom_call_target="tpu_custom_call" | custom-call | tf_op jit(solution)/shard_map/step/pallas_call | solution.py:460
  35.8 0.9 %publish.1 = (bf16[1,20,128,128]{3,2,1,0:T(8,128)(2,1)}, f32[20,36]{1,0:T(8,128)}) custom-call(bf16[1,20,128,128]{3,2,1,0:T(8,128)(2,1)S(1)} %get-tuple-element.4.fg, f32[20,36]{1,0:T(8,128)S(1)} %get-tuple-element.5.wg), custom_call_target="tpu_custom_call" | custom-call | tf_op jit(solution)/shard_map/publish/pallas_call | solution.py:507
